TPU v7x, 256 devices: a whole 4x4x8 slice. The times are simulated.
256 devices in a mesh: dp: 4 (over x), rad: 8 (over y, z_lo), azi: 8 (over z_hi, core).
Axes of the slice: x: 4, y: 4, z: 8 (z_hi: 4, z_lo: 2; z = z_hi * 2 + z_lo), core: 2. Of those that a mesh axis runs over, the one named last changes fastest.
Arguments:
- inputs: bfloat16 [4, 96, 32, 64, 256], P('dp', None, 'rad', 'azi'), may hold values from -6 to 6
- weight: bfloat16 [96, 2592], P('dp'), may hold values from -0.125 to 0.125
- bias: bfloat16 [96], P('dp'), may hold values from -3 to 3
- cotangent: bfloat16 [4, 96, 32, 64, 256], P('dp', None, 'rad', 'azi'), may hold values from -6 to 6
Outputs:
- output: bfloat16 [4, 96, 32, 64, 256], P('dp', None, 'rad', 'azi')
- input_grad: bfloat16 [4, 96, 32, 64, 256], P('dp', None, 'rad', 'azi')
- weight_grad: float32 [96, 2592], P('dp')
- bias_grad: float32 [96], P('dp')
All inputs are finite; a program needn't handle non-finite values.
Results may differ from a plain program's by a relative error of at most 0.015.
Values may be sent and summed in bfloat16 or wider, within the bound.
No kernel may reach another device: no remote copies, remote signals or barrier semaphores. Data moves between devices by JAX's collectives and lax.ppermute only.
A program may use at most 128 MiB of HBM per device.

v0:
```python
import jax
import jax.numpy as jnp
from jax import lax
from jax.sharding import PartitionSpec as P

inverse_scale = 1.0 / 1024.0


def with_halo(cells, sides, width):
    for axis, dim in sides:
        count = lax.axis_size(axis)
        head = lax.slice_in_dim(cells, 0, width, axis=dim)
        tail = lax.slice_in_dim(cells, cells.shape[dim] - width, cells.shape[dim], axis=dim)
        cells = jnp.concatenate(
            [
                lax.ppermute(tail, axis, [(i, (i + 1) % count) for i in range(count)]),
                cells,
                lax.ppermute(head, axis, [((i + 1) % count, i) for i in range(count)]),
            ],
            axis=dim,
        )
    return cells


def rim_fix(extended):
    rad_index = lax.axis_index("rad")
    rad_last = lax.axis_size("rad") - 1
    low_rim = jnp.where(rad_index > 0, extended[:, :, :1], jnp.zeros_like(extended[:, :, :1]))
    high_rim = jnp.where(
        rad_index < rad_last, extended[:, :, -1:], jnp.zeros_like(extended[:, :, -1:])
    )
    return jnp.concatenate([low_rim, extended[:, :, 1:-1], high_rim], axis=2)


def axial_pad(extended):
    return jnp.pad(extended, ((0, 0), (0, 0), (0, 0), (0, 0), (1, 1)))


def extend_input(field):
    extended = rim_fix(with_halo(field, (("rad", 2), ("azi", 3)), 1))
    return axial_pad(extended)


def extend_grad(field):
    extended = rim_fix(with_halo(field, (("rad", 2), ("azi", 3)), 1))
    return axial_pad(extended)


def convolve(left, right, numbers):
    return lax.conv_general_dilated(
        left,
        right,
        (1, 1, 1),
        "VALID",
        dimension_numbers=numbers,
        preferred_element_type=jnp.float32,
    )


def on_device(inputs, weight, bias, cotangent):
    channels = inputs.shape[1]
    full_weight, full_bias = (
        lax.all_gather(weight, "dp", axis=0, tiled=True),
        lax.all_gather(bias, "dp", axis=0, tiled=True),
    )
    out_rows = full_weight.shape[0]
    kernel_taps = full_weight.reshape(out_rows, 3, 3, 3, channels)
    kernel_fwd = kernel_taps.transpose(0, 4, 1, 2, 3)
    kernel_back = kernel_taps[:, ::-1, ::-1, ::-1, :].transpose(4, 0, 1, 2, 3)
    padded = extend_input(inputs)
    preact = convolve(padded, kernel_fwd, ("NCDHW", "OIDHW", "NCDHW"))
    preact = preact + full_bias.astype(jnp.float32)[None, :, None, None, None]
    gate_value = jax.nn.sigmoid(preact)
    output = (preact * gate_value).astype(jnp.bfloat16)
    delta_z = (
        cotangent.astype(jnp.float32) * gate_value * (1.0 + preact * (1.0 - gate_value))
    ).astype(jnp.bfloat16)
    delta_pad = extend_grad(delta_z)
    backward = convolve(delta_pad, kernel_back, ("NCDHW", "OIDHW", "NCDHW"))
    kernel_grad = convolve(padded, delta_z, ("CNDHW", "IODHW", "NCDHW"))
    weight_term = (
        kernel_grad.transpose(1, 2, 3, 4, 0).reshape(out_rows, 27 * channels) * inverse_scale
    )
    bias_term = jnp.sum(delta_z.astype(jnp.float32), axis=(0, 2, 3, 4)) * inverse_scale
    group_part = (
        lax.psum_scatter(
            weight_term.astype(jnp.bfloat16), "dp", scatter_dimension=0, tiled=True
        ).astype(jnp.float32),
        lax.psum_scatter(
            bias_term.astype(jnp.bfloat16), "dp", scatter_dimension=0, tiled=True
        ).astype(jnp.float32),
    )
    weight_grad, bias_grad = lax.psum((group_part[0], group_part[1]), ("rad", "azi"))
    return (output, backward.astype(jnp.bfloat16), weight_grad, bias_grad)


def solution(mesh):
    return jax.shard_map(
        on_device,
        mesh=mesh,
        in_specs=(
            P("dp", None, "rad", "azi", None),
            P("dp", None),
            P("dp"),
            P("dp", None, "rad", "azi", None),
        ),
        out_specs=(
            P("dp", None, "rad", "azi", None),
            P("dp", None, "rad", "azi", None),
            P("dp", None),
            P("dp"),
        ),
        check_vma=False,
    )
```

profile of v0, /device:TPU:2, one launch (start us, length us, event | category | flops | bytes accessed | tf_op | source)
XLA Modules:
  0.0 530.9 jit_solution(4180190173391444999)
XLA Ops:
  8.4 4.4 collective-permute-start.1
  12.8 9.5 %collective-permute-done.1 = bf16[1,96,1,8,256]{4,3,2,1,0:T(8,128)(2,1)S(1)} collective-permute-done((bf16[1,96,1,8,256]{4,3,2,1,0:T(8,128)(2,1)S(1)}, bf16[1,96,1,8,256]{4,3,2,1,0:T(8,128)(2,1)S(1)}, u32[]{:S(2)}, u32[]{:S(2)}) %collective-permute-start.1) | collective-permute-done | bytes 393248 | tf_op jit(solution)/shard_map/ppermute | solution.py:18
  22.3 8.0 %collective-permute-done = bf16[1,96,1,8,256]{4,3,2,1,0:T(8,128)(2,1)S(1)} collective-permute-done((bf16[1,96,1,8,256]{4,3,2,1,0:T(8,128)(2,1)S(1)}, bf16[1,96,1,8,256]{4,3,2,1,0:T(8,128)(2,1)S(1)}, u32[]{:S(2)}, u32[]{:S(2)}) %collective-permute-start) | collective-permute-done | bytes 393248 | tf_op jit(solution)/shard_map/ppermute | solution.py:16
  30.4 1.7 pad_maximum_fusion.3
  35.1 8.6 %all-reduce = bf16[96]{0:T(256)(128)(2,1)S(1)} all-reduce(bf16[96]{0:T(256)(128)(2,1)S(1)} %dynamic-update-slice), channel_id=1, replica_groups=mesh['dp'=4,'rad'=8,'azi'=8] {'dp'}, use_global_device_ids=true, to_apply=%add | all-reduce | flops 96 | bytes 384
  43.8 12.8 %all_gather.6 = bf16[96,2592]{1,0:T(8,128)(2,1)S(1)} all-gather(bf16[24,2592]{1,0:T(8,128)(2,1)} %param.5), channel_id=1, replica_groups=mesh['dp'=4,'rad'=8,'azi'=8] {'dp'}, dimensions={0}, use_global_device_ids=true | all-gather | bytes 622080 | tf_op jit(solution)/shard_map/all_gather | solution.py:63
  57.7 4.6 copy.69
  65.7 5.6 %collective-permute-done.3 = bf16[1,96,6,1,256]{4,1,3,2,0:T(8,128)(2,1)S(1)} collective-permute-done((bf16[1,96,6,1,256]{4,1,3,2,0:T(8,128)(2,1)S(1)}, bf16[1,96,6,1,256]{4,1,3,2,0:T(8,128)(2,1)S(1)}, u32[]{:S(2)}, u32[]{:S(2)}) %collective-permute-start.3) | collective-permute-done | bytes 294944 | tf_op jit(solution)/shard_map/ppermute | solution.py:18
  71.5 1.8 pad_maximum_fusion.1
  73.4 3.6 copy.88
  77.0 5.5 %pad.3.clone = bf16[96,6,10,1,264]{0,4,2,1,3:T(8,128)(2,1)} pad(bf16[96,6,10,1,256]{0,4,2,1,3:T(8,128)(2,1)} %copy.88, bf16[]{:T(256)} %constant.6.clone.1), padding=0_0x0_0x0_0x0_0x1_7 | pad | bytes 5990402 | tf_op jit(solution)/shard_map/concatenate | solution.py:32
  82.5 7.2 %reshape.21 = bf16[96,6,10,1,8,33]{0,5,4,2,1,3:T(8,128)(2,1)} reshape(bf16[96,6,10,1,264]{0,4,2,1,3:T(8,128)(2,1)} %pad.3.clone) | data formatting | bytes 6082560 | tf_op jit(solution)/shard_map/conv_general_dilated | solution.py:50
  89.7 3.1 copy.66
  92.9 17.9 %add_divide_fusion = (f32[4,8,8,33,96]{4,2,3,1,0:T(8,128)S(1)}, bf16[4,8,8,33,96]{4,2,3,1,0:T(8,128)(2,1)}, f32[4,8,8,33,96]{4,2,3,1,0:T(8,128)S(1)}) fusion(f32[96]{0:T(128)S(1)} %convert_element_type.36, pred[8,33]{0,1:T(8,128)(4,1)S(1)} %copy-done.8, bf16[96,3,3,3,96]{0,4,3,2,1:T(8,128)(2,1)S(1)} %bitcast.55, ...), kind=kOutput, calls=%fused_computation.6 | convolution fusion | flops 4222052352 | bytes 11810952 | tf_op jit(solution)/shard_map/conv_general_dilated | solution.py:50
  113.2 1.6 convert_reduce_fusion
  117.4 2.0 collective-permute-start.4
  119.4 16.3 %copy.83 = bf16[1,96,6,10,256]{1,0,4,3,2:T(2,128)(2,1)} copy(bf16[1,96,6,10,256]{4,1,3,2,0:T(8,128)(2,1)} %get-tuple-element.25) | data formatting | bytes 5898240 | tf_op jit(solution)/shard_map/concatenate | solution.py:32
  135.8 63.2 %fusion.28 = bf16[96,3,3,3,96]{0,4,3,2,1:T(8,128)(2,1)S(1)} fusion(bf16[1,96,6,10,256]{1,0,4,3,2:T(2,128)(2,1)} %copy.83, bf16[1,96,4,8,256]{1,3,4,2,0:T(8,128)(2,1)S(1)} %get-tuple-element.19), kind=kOutput, calls=%fused_computation.38 | convolution fusion | flops 4066744320 | bytes 5019648 | tf_op jit(solution)/shard_map/transpose | solution.py:82
  200.7 4.6 copy.86
  206.4 1.5 copy.75
  208.0 1.5 copy.74
  210.3 1.6 copy-done
  213.6 3.8 collective-permute-start.7
  218.0 11.4 %all-reduce.2 = bf16[96]{0:T(256)(128)(2,1)S(1)} all-reduce(bf16[96]{0:T(256)(128)(2,1)S(1)} %multiply_convert_fusion.1), channel_id=3, replica_groups=mesh['dp'=4,'rad'=8,'azi'=8] {'dp'}, use_global_device_ids=true, to_apply=%region_3.4.clone | all-reduce | flops 96 | bytes 384
  229.5 3.7 copy.78
  234.3 3.7 copy.89
  238.0 5.4 %pad.5.clone = bf16[96,6,10,1,264]{0,4,2,1,3:T(8,128)(2,1)} pad(bf16[96,6,10,1,256]{0,4,2,1,3:T(8,128)(2,1)} %copy.89, bf16[]{:T(256)} %constant.6.clone.1), padding=0_0x0_0x0_0x0_0x1_7 | pad | bytes 5990402 | tf_op jit(solution)/shard_map/concatenate | solution.py:32
  243.4 7.2 %reshape.28 = bf16[96,6,10,1,8,33]{0,5,4,2,1,3:T(8,128)(2,1)} reshape(bf16[96,6,10,1,264]{0,4,2,1,3:T(8,128)(2,1)} %pad.5.clone) | data formatting | bytes 6082560 | tf_op jit(solution)/shard_map/conv_general_dilated | solution.py:50
  250.7 3.1 copy.81
  253.9 15.8 %select_convert_fusion = bf16[4,8,8,33,96]{4,2,3,1,0:T(8,128)(2,1)S(1)} fusion(pred[8,33]{0,1:T(8,128)(4,1)S(1)} %copy-done.9, bf16[96,3,3,3,96]{0,4,3,2,1:T(8,128)(2,1)S(1)} %bitcast.56, bf16[96,6,10,1,7,2]{0,4,5,2,1,3:T(8,128)(2,1)S(1)} %slice.76, bf16[96,6,10,1,8,33]{0,4,5,2,1,3:T(8,128)(2,1)S(1)} %copy.81), kind=kOutput, calls=%fused_computation.3 | convolution fusion | flops 4215564288 | bytes 5322504 | tf_op jit(solution)/shard_map/conv_general_dilated | solution.py:50
  270.1 3.0 copy.87
  273.1 250.6 %all-reduce.5 = (f32[24,2592]{1,0:T(8,128)}, f32[24]{0:T(128)}) all-reduce(bf16[24,2592]{1,0:T(8,128)(2,1)} %reduce-scatter.4.cloned.1.call-done, f32[24]{0:T(128)S(1)} %dynamic-slice_convert_fusion), channel_id=1, replica_groups=mesh['dp'=4,'rad'=8,'azi'=8] {'rad','azi'}, use_global_device_ids=true, to_apply=%region_1.2 | all-reduce | flops 62232 | bytes 373440 | tf_op jit(solution)/shard_map/psum | solution.py:93
  (68 shorter events, 20.0 us)
Async XLA Ops:
  7.2 265.9 %reduce-scatter.4.cloned.1.call-start = ((), (), s32[]{:S(2)}) async-start(), calls=%async_computation.1 | async-start | bytes 645120
  8.4 13.9 %collective-permute-start.1 = (bf16[1,96,1,8,256]{4,3,2,1,0:T(8,128)(2,1)S(1)}, bf16[1,96,1,8,256]{4,3,2,1,0:T(8,128)(2,1)S(1)}, u32[]{:S(2)}, u32[]{:S(2)}) collective-permute-start(bf16[1,96,1,8,256]{4,3,2,1,0:T(8,128)(2,1)S(1)} %get-tuple-element.36), channel_id=1, source_target_pairs={{8,0},{16,8},{24,16},{32,24},{40,32},{48,40},{56,48},{0,56},{9,1},... | collective-permute-start | bytes 1179656 | tf_op jit(solution)/shard_map/ppermute | solution.py:18
  12.8 20.8 %copy-start.5 = (u32[256]{0:T(256)S(1)}, u32[256]{0:T(256)}, u32[]{:S(2)}) copy-start(u32[256]{0:T(256)} %constant.33) | copy-start | bytes 3076
  12.8 22.0 %copy-start.7 = (bf16[24]{0:T(256)(128)(2,1)S(1)}, bf16[24]{0:T(256)(128)(2,1)}, u32[]{:S(2)}) copy-start(bf16[24]{0:T(256)(128)(2,1)} %param.6) | copy-start | bytes 148
  12.8 17.5 %collective-permute-start = (bf16[1,96,1,8,256]{4,3,2,1,0:T(8,128)(2,1)S(1)}, bf16[1,96,1,8,256]{4,3,2,1,0:T(8,128)(2,1)S(1)}, u32[]{:S(2)}, u32[]{:S(2)}) collective-permute-start(bf16[1,96,1,8,256]{4,3,2,1,0:T(8,128)(2,1)S(1)} %get-tuple-element.35), channel_id=1, source_target_pairs={{0,8},{8,16},{16,24},{24,32},{32,40},{40,48},{48,56},{56,0},{1,9},... | collective-permute-start | bytes 1179656 | tf_op jit(solution)/shard_map/ppermute | solution.py:16
  33.6 30.3 %collective-permute-start.2 = (bf16[1,96,6,1,256]{4,1,3,2,0:T(8,128)(2,1)}, bf16[1,96,6,1,256]{4,1,3,2,0:T(8,128)(2,1)}, u32[]{:S(2)}, u32[]{:S(2)}) collective-permute-start(bf16[1,96,6,1,256]{4,1,3,2,0:T(8,128)(2,1)} %copy.97), channel_id=1, source_target_pairs={{0,1},{1,2},{2,3},{3,4},{4,5},{5,6},{6,7},{7,0},{8,9},{9,10},{10,1... | collective-permute-start | bytes 884744 | tf_op jit(solution)/shard_map/ppermute | solution.py:16
  63.0 8.3 %collective-permute-start.3 = (bf16[1,96,6,1,256]{4,1,3,2,0:T(8,128)(2,1)S(1)}, bf16[1,96,6,1,256]{4,1,3,2,0:T(8,128)(2,1)S(1)}, u32[]{:S(2)}, u32[]{:S(2)}) collective-permute-start(bf16[1,96,6,1,256]{4,1,3,2,0:T(8,128)(2,1)S(1)} %copy.98), channel_id=1, source_target_pairs={{1,0},{2,1},{3,2},{4,3},{5,4},{6,5},{7,6},{0,7},{9,8},{10,9},{11,1... | collective-permute-start | bytes 884744 | tf_op jit(solution)/shard_map/ppermute | solution.py:18
  89.7 3.2 copy-start.3
  89.7 3.2 copy-start.8
  111.6 1.6 copy-start.1
  116.2 90.3 %collective-permute-start.5 = (bf16[1,96,1,8,256]{4,3,2,1,0:T(8,128)(2,1)}, bf16[1,96,1,8,256]{4,3,2,1,0:T(8,128)(2,1)}, u32[]{:S(2)}, u32[]{:S(2)}) collective-permute-start(bf16[1,96,1,8,256]{4,3,2,1,0:T(8,128)(2,1)} %copy.73), channel_id=1, source_target_pairs={{8,0},{16,8},{24,16},{32,24},{40,32},{48,40},{56,48},{0,56},{9,1},... | collective-permute-start | bytes 1179656 | tf_op jit(solution)/shard_map/ppermute | solution.py:18
  117.4 90.6 %collective-permute-start.4 = (bf16[1,96,1,8,256]{4,3,2,1,0:T(8,128)(2,1)}, bf16[1,96,1,8,256]{4,3,2,1,0:T(8,128)(2,1)}, u32[]{:S(2)}, u32[]{:S(2)}) collective-permute-start(bf16[1,96,1,8,256]{4,3,2,1,0:T(8,128)(2,1)} %copy.72), channel_id=1, source_target_pairs={{0,8},{8,16},{16,24},{24,32},{32,40},{40,48},{48,56},{56,0},{1,9},... | collective-permute-start | bytes 1179656 | tf_op jit(solution)/shard_map/ppermute | solution.py:16
  135.8 63.2 %copy-start.2 = (bf16[4,8,8,33,96]{4,2,3,1,0:T(8,128)(2,1)S(1)}, bf16[4,8,8,33,96]{4,2,3,1,0:T(8,128)(2,1)}, u32[]{:S(2)}) copy-start(bf16[4,8,8,33,96]{4,2,3,1,0:T(8,128)(2,1)} %get-tuple-element.21) | copy-start | bytes 4866052
  210.3 1.6 copy-start
  211.9 6.1 %copy-start.6 = (f32[96]{0:T(128)S(1)}, f32[96]{0:T(128)}, u32[]{:S(2)}) copy-start(f32[96]{0:T(128)} %get-tuple-element.18) | copy-start | bytes 1156
  213.6 19.7 %collective-permute-start.7 = (bf16[1,96,6,1,256]{4,1,3,2,0:T(8,128)(2,1)S(1)}, bf16[1,96,6,1,256]{4,1,3,2,0:T(8,128)(2,1)S(1)}, u32[]{:S(2)}, u32[]{:S(2)}) collective-permute-start(bf16[1,96,6,1,256]{4,1,3,2,0:T(8,128)(2,1)S(1)} %copy.77), channel_id=1, source_target_pairs={{1,0},{2,1},{3,2},{4,3},{5,4},{6,5},{7,6},{0,7},{9,8},{10,9},{11,1... | collective-permute-start | bytes 884744 | tf_op jit(solution)/shard_map/ppermute | solution.py:18
  217.9 15.4 %collective-permute-start.6 = (bf16[1,96,6,1,256]{4,1,3,2,0:T(8,128)(2,1)S(1)}, bf16[1,96,6,1,256]{4,1,3,2,0:T(8,128)(2,1)S(1)}, u32[]{:S(2)}, u32[]{:S(2)}) collective-permute-start(bf16[1,96,6,1,256]{4,1,3,2,0:T(8,128)(2,1)S(1)} %copy.76), channel_id=1, source_target_pairs={{0,1},{1,2},{2,3},{3,4},{4,5},{5,6},{6,7},{7,0},{8,9},{9,10},{10,1... | collective-permute-start | bytes 884744 | tf_op jit(solution)/shard_map/ppermute | solution.py:16
  250.7 3.2 copy-start.4
  250.7 3.2 copy-start.9
Sparse Core Ops, SparseCore 0:
  206.6 25.3 reduce-scatter.3
where the time goes:
time: 537 us; the launch traced here: 531 us
  blocking collectives  283 us (53%)
  matrix products  96.9 us (18%)
  local copies, waits for them, and re-layouts  93.1 us (17%)
  waiting for transfers between devices  23.2 us (4%)
  between operations  16.1 us (3%)
  starting transfers between devices  11.3 us (2%)
  other arithmetic  6.9 us (1%)
    psum x1, blocking collectives, on_device(): lax.psum((group_part[0], group_part[1]), ('rad', 'azi'))  251 us
    transpose x1, matrix products, on_device(): kernel_grad.transpose(1, 2, 3, 4, 0).reshape(out_rows, 27 * channels)  63.2 us
    conv_general_dilated x2, matrix products, convolve(): lax.conv_general_dilated(left, right, (1, 1, 1), 'VALID', dimension_numbe...  33.7 us
    concatenate x3, local copies, waits for them, and re-layouts, rim_fix(): return jnp.concatenate([low_rim, extended[:, :, 1:-1], high_rim], axis=2)  27.2 us
    unnamed x32, local copies, waits for them, and re-layouts  25.5 us
    conv_general_dilated x6, local copies, waits for them, and re-layouts, convolve(): lax.conv_general_dilated(left, right, (1, 1, 1), 'VALID', dimension_numbe...  20.8 us
    unnamed x2, blocking collectives  20.1 us
    ppermute x4, waiting for transfers between devices, with_halo(): lax.ppermute(head, axis, [((i + 1) % count, i) for i in range(count)])  15.1 us
  transfers between devices with their start and end apart: 9, of which 3 were waited for; matrix products, arithmetic and copies ran while one was open for 28% of the time, Pallas kernels for 0%

commit v1 on v0

--- a/solution.py
+++ b/solution.py
@@ -90,7 +90,7 @@
             bias_term.astype(jnp.bfloat16), "dp", scatter_dimension=0, tiled=True
         ).astype(jnp.float32),
     )
-    weight_grad, bias_grad = lax.psum((group_part[0], group_part[1]), ("rad", "azi"))
+    weight_grad, bias_grad = lax.psum(lax.psum((group_part[0], group_part[1]), "azi"), "rad")
     return (output, backward.astype(jnp.bfloat16), weight_grad, bias_grad)
 
 

time: 537 us -> 397 us (0.74)
  blocking collectives: 283 us -> 85.6 us
  waiting for transfers between devices: 23.2 us -> 76.2 us
    psum x1 -> x2, blocking collectives: 251 us -> 52.8 us  [the longest x1 33.5 us: on_device(): lax.psum((group_part[0], group_part[1]), 'azi')]
    psum x0 -> x1, waiting for transfers between devices: none -> 53 us  [on_device(): lax.psum(lax.psum((group_part[0], group_part[1]), 'azi'), 'rad')]
    unnamed x32 -> x33, local copies, waits for them, and re-layouts: 25.5 us -> 28.8 us
  transfers between devices with their start and end apart: 9 -> 10, of which waited for: 3 -> 4; matrix products, arithmetic and copies ran while one was open for 28% -> 38% of each run, Pallas kernels for 0% -> 0%
where the time goes in v1:
time: 397 us; the launch traced here: 391 us
  local copies, waits for them, and re-layouts  97.8 us (25%)
  matrix products  96.9 us (24%)
  blocking collectives  85.6 us (22%)
  waiting for transfers between devices  76.2 us (19%)
  between operations  16.2 us (4%)
  starting transfers between devices  11.3 us (3%)
  other arithmetic  6.91 us (2%)
    transpose x1, matrix products, on_device(): kernel_grad.transpose(1, 2, 3, 4, 0).reshape(out_rows, 27 * channels)  63.2 us
    psum x1, waiting for transfers between devices, on_device(): lax.psum(lax.psum((group_part[0], group_part[1]), 'azi'), 'rad')  53 us
    conv_general_dilated x2, matrix products, convolve(): lax.conv_general_dilated(left, right, (1, 1, 1), 'VALID', dimension_numbe...  33.7 us
    psum x1, blocking collectives, on_device(): lax.psum((group_part[0], group_part[1]), 'azi')  33.5 us
    unnamed x33, local copies, waits for them, and re-layouts  28.8 us
    concatenate x3, local copies, waits for them, and re-layouts, rim_fix(): return jnp.concatenate([low_rim, extended[:, :, 1:-1], high_rim], axis=2)  27.3 us
    conv_general_dilated x6, local copies, waits for them, and re-layouts, convolve(): lax.conv_general_dilated(left, right, (1, 1, 1), 'VALID', dimension_numbe...  20.8 us
    unnamed x2, blocking collectives  20.1 us
  transfers between devices with their start and end apart: 10, of which 4 were waited for; matrix products, arithmetic and copies ran while one was open for 38% of the time, Pallas kernels for 0%

profile of v1, /device:TPU:2, one launch (start us, length us, event | category | flops | bytes accessed | tf_op | source)
XLA Modules:
  0.0 390.9 jit_solution(5605781075550409405)
XLA Ops:
  8.4 4.4 %collective-permute-start.1 = (bf16[1,96,1,8,256]{4,3,2,1,0:T(8,128)(2,1)S(1)}, bf16[1,96,1,8,256]{4,3,2,1,0:T(8,128)(2,1)S(1)}, u32[]{:S(2)}, u32[]{:S(2)}) collective-permute-start(bf16[1,96,1,8,256]{4,3,2,1,0:T(8,128)(2,1)S(1)} %get-tuple-element.36), channel_id=1, source_target_pairs={{8,0},{16,8},{24,16},{32,24},{40,32},{48,40},{56,48},{0,56},{9,1},... | collective-permute-start | bytes 1179656 | tf_op jit(solution)/shard_map/ppermute | solution.py:18
  12.8 9.5 %collective-permute-done.1 = bf16[1,96,1,8,256]{4,3,2,1,0:T(8,128)(2,1)S(1)} collective-permute-done((bf16[1,96,1,8,256]{4,3,2,1,0:T(8,128)(2,1)S(1)}, bf16[1,96,1,8,256]{4,3,2,1,0:T(8,128)(2,1)S(1)}, u32[]{:S(2)}, u32[]{:S(2)}) %collective-permute-start.1) | collective-permute-done | bytes 393248 | tf_op jit(solution)/shard_map/ppermute | solution.py:18
  22.3 8.0 %collective-permute-done = bf16[1,96,1,8,256]{4,3,2,1,0:T(8,128)(2,1)S(1)} collective-permute-done((bf16[1,96,1,8,256]{4,3,2,1,0:T(8,128)(2,1)S(1)}, bf16[1,96,1,8,256]{4,3,2,1,0:T(8,128)(2,1)S(1)}, u32[]{:S(2)}, u32[]{:S(2)}) %collective-permute-start) | collective-permute-done | bytes 393248 | tf_op jit(solution)/shard_map/ppermute | solution.py:16
  30.4 1.7 pad_maximum_fusion.3
  35.1 8.6 %all-reduce = bf16[96]{0:T(256)(128)(2,1)S(1)} all-reduce(bf16[96]{0:T(256)(128)(2,1)S(1)} %dynamic-update-slice), channel_id=1, replica_groups=mesh['dp'=4,'rad'=8,'azi'=8] {'dp'}, use_global_device_ids=true, to_apply=%add | all-reduce | flops 96 | bytes 384
  43.8 12.8 %all_gather.6 = bf16[96,2592]{1,0:T(8,128)(2,1)S(1)} all-gather(bf16[24,2592]{1,0:T(8,128)(2,1)} %param.5), channel_id=1, replica_groups=mesh['dp'=4,'rad'=8,'azi'=8] {'dp'}, dimensions={0}, use_global_device_ids=true | all-gather | bytes 622080 | tf_op jit(solution)/shard_map/all_gather | solution.py:63
  57.7 4.6 %copy.69 = bf16[1,96,4,8,256]{1,3,4,2,0:T(8,128)(2,1)} copy(bf16[1,96,4,8,256]{4,3,2,1,0:T(8,128)(2,1)} %param.7) | data formatting | bytes 3145728 | tf_op args[3]
  65.7 5.6 %collective-permute-done.3 = bf16[1,96,6,1,256]{4,1,3,2,0:T(8,128)(2,1)S(1)} collective-permute-done((bf16[1,96,6,1,256]{4,1,3,2,0:T(8,128)(2,1)S(1)}, bf16[1,96,6,1,256]{4,1,3,2,0:T(8,128)(2,1)S(1)}, u32[]{:S(2)}, u32[]{:S(2)}) %collective-permute-start.3) | collective-permute-done | bytes 294944 | tf_op jit(solution)/shard_map/ppermute | solution.py:18
  71.6 1.8 pad_maximum_fusion.1
  73.4 3.7 copy.88
  77.1 5.5 %pad.3.clone = bf16[96,6,10,1,264]{0,4,2,1,3:T(8,128)(2,1)} pad(bf16[96,6,10,1,256]{0,4,2,1,3:T(8,128)(2,1)} %copy.88, bf16[]{:T(256)} %constant.6.clone.1), padding=0_0x0_0x0_0x0_0x1_7 | pad | bytes 5990402 | tf_op jit(solution)/shard_map/concatenate | solution.py:32
  82.6 7.2 %reshape.21 = bf16[96,6,10,1,8,33]{0,5,4,2,1,3:T(8,128)(2,1)} reshape(bf16[96,6,10,1,264]{0,4,2,1,3:T(8,128)(2,1)} %pad.3.clone) | data formatting | bytes 6082560 | tf_op jit(solution)/shard_map/conv_general_dilated | solution.py:50
  89.8 3.1 copy.66
  93.0 18.0 %add_divide_fusion = (f32[4,8,8,33,96]{4,2,3,1,0:T(8,128)S(1)}, bf16[4,8,8,33,96]{4,2,3,1,0:T(8,128)(2,1)}, f32[4,8,8,33,96]{4,2,3,1,0:T(8,128)S(1)}) fusion(f32[96]{0:T(128)S(1)} %convert_element_type.36, pred[8,33]{0,1:T(8,128)(4,1)S(1)} %copy-done.8, bf16[96,3,3,3,96]{0,4,3,2,1:T(8,128)(2,1)S(1)} %bitcast.55, ...), kind=kOutput, calls=%fused_computation.6 | convolution fusion | flops 4222052352 | bytes 11810952 | tf_op jit(solution)/shard_map/conv_general_dilated | solution.py:50
  117.5 2.0 collective-permute-start.4
  119.5 16.4 %copy.83 = bf16[1,96,6,10,256]{1,0,4,3,2:T(2,128)(2,1)} copy(bf16[1,96,6,10,256]{4,1,3,2,0:T(8,128)(2,1)} %get-tuple-element.25) | data formatting | bytes 5898240 | tf_op jit(solution)/shard_map/concatenate | solution.py:32
  135.9 63.2 %fusion.28 = bf16[96,3,3,3,96]{0,4,3,2,1:T(8,128)(2,1)S(1)} fusion(bf16[1,96,6,10,256]{1,0,4,3,2:T(2,128)(2,1)} %copy.83, bf16[1,96,4,8,256]{1,3,4,2,0:T(8,128)(2,1)S(1)} %get-tuple-element.19), kind=kOutput, calls=%fused_computation.38 | convolution fusion | flops 4066744320 | bytes 5019648 | tf_op jit(solution)/shard_map/transpose | solution.py:82
  200.9 4.6 %copy.86 = bf16[1,96,4,8,256]{4,3,2,1,0:T(8,128)(2,1)} copy(bf16[1,96,4,8,256]{1,3,4,2,0:T(8,128)(2,1)} %slice_bitcast_fusion.3) | data formatting | bytes 3145728
  210.5 1.6 copy-done
  213.8 3.8 collective-permute-start.7
  218.2 11.4 %all-reduce.2 = bf16[96]{0:T(256)(128)(2,1)S(1)} all-reduce(bf16[96]{0:T(256)(128)(2,1)S(1)} %multiply_convert_fusion.1), channel_id=3, replica_groups=mesh['dp'=4,'rad'=8,'azi'=8] {'dp'}, use_global_device_ids=true, to_apply=%region_4.5.clone | all-reduce | flops 96 | bytes 384
  229.7 3.7 copy.78
  234.5 3.7 copy.89
  238.2 5.4 %pad.5.clone = bf16[96,6,10,1,264]{0,4,2,1,3:T(8,128)(2,1)} pad(bf16[96,6,10,1,256]{0,4,2,1,3:T(8,128)(2,1)} %copy.89, bf16[]{:T(256)} %constant.6.clone.1), padding=0_0x0_0x0_0x0_0x1_7 | pad | bytes 5990402 | tf_op jit(solution)/shard_map/concatenate | solution.py:32
  243.6 7.2 %reshape.28 = bf16[96,6,10,1,8,33]{0,5,4,2,1,3:T(8,128)(2,1)} reshape(bf16[96,6,10,1,264]{0,4,2,1,3:T(8,128)(2,1)} %pad.5.clone) | data formatting | bytes 6082560 | tf_op jit(solution)/shard_map/conv_general_dilated | solution.py:50
  250.8 3.1 copy.81
  254.0 15.8 %select_convert_fusion = bf16[4,8,8,33,96]{4,2,3,1,0:T(8,128)(2,1)S(1)} fusion(pred[8,33]{0,1:T(8,128)(4,1)S(1)} %copy-done.9, bf16[96,3,3,3,96]{0,4,3,2,1:T(8,128)(2,1)S(1)} %bitcast.56, bf16[96,6,10,1,7,2]{0,4,5,2,1,3:T(8,128)(2,1)S(1)} %slice.76, bf16[96,6,10,1,8,33]{0,4,5,2,1,3:T(8,128)(2,1)S(1)} %copy.81), kind=kOutput, calls=%fused_computation.3 | convolution fusion | flops 4215564288 | bytes 5322504 | tf_op jit(solution)/shard_map/conv_general_dilated | solution.py:50
  270.1 33.5 %all-reduce.8 = (f32[24,2592]{1,0:T(8,128)}, f32[24]{0:T(128)S(1)}) all-reduce(bf16[24,2592]{1,0:T(8,128)(2,1)} %reduce-scatter.4.cloned.1.call-done, f32[24]{0:T(128)S(1)} %dynamic-slice_convert_fusion), channel_id=1, replica_groups=mesh['dp'=4,'rad'=8,'azi'=8] {'azi'}, use_global_device_ids=true, to_apply=%region_1.2 | all-reduce | flops 62232 | bytes 373440 | tf_op jit(solution)/shard_map/psum | solution.py:93
  305.1 4.6 %copy.87 = bf16[1,96,4,8,256]{4,3,2,1,0:T(8,128)(2,1)} copy(bf16[1,96,4,8,256]{1,3,4,2,0:T(8,128)(2,1)} %slice_bitcast_fusion.2) | data formatting | bytes 3145728
  309.8 19.3 %psum.31 = f32[24]{0:T(128)} all-reduce(f32[24]{0:T(128)S(1)} %get-tuple-element.17), channel_id=1, replica_groups=mesh['dp'=4,'rad'=8,'azi'=8] {'rad'}, use_global_device_ids=true, to_apply=%region_6.7 | all-reduce | flops 24 | bytes 192 | tf_op jit(solution)/shard_map/psum | solution.py:93
  329.0 53.0 %all-reduce.7.cloned.1.call-done = f32[24,2592]{1,0:T(8,128)} async-done(((f32[24,2592]{1,0:T(8,128)}), f32[24,2592]{1,0:T(8,128)}) %all-reduce.7.cloned.1.call-update) | async-done | bytes 248848 | tf_op jit(solution)/shard_map/psum | solution.py:93
  382.0 1.7 copy.106
  (73 shorter events, 26.1 us)
Async XLA Ops:
  7.2 263.0 %reduce-scatter.4.cloned.1.call-start = ((), (), s32[]{:S(2)}) async-start(), calls=%async_computation.2 | async-start | bytes 645120
  8.4 13.9 %collective-permute-start.1 = (bf16[1,96,1,8,256]{4,3,2,1,0:T(8,128)(2,1)S(1)}, bf16[1,96,1,8,256]{4,3,2,1,0:T(8,128)(2,1)S(1)}, u32[]{:S(2)}, u32[]{:S(2)}) collective-permute-start(bf16[1,96,1,8,256]{4,3,2,1,0:T(8,128)(2,1)S(1)} %get-tuple-element.36), channel_id=1, source_target_pairs={{8,0},{16,8},{24,16},{32,24},{40,32},{48,40},{56,48},{0,56},{9,1},... | collective-permute-start | bytes 1179656 | tf_op jit(solution)/shard_map/ppermute | solution.py:18
  12.8 20.8 %copy-start.5 = (u32[256]{0:T(256)S(1)}, u32[256]{0:T(256)}, u32[]{:S(2)}) copy-start(u32[256]{0:T(256)} %constant.33) | copy-start | bytes 3076
  12.8 22.0 %copy-start.7 = (bf16[24]{0:T(256)(128)(2,1)S(1)}, bf16[24]{0:T(256)(128)(2,1)}, u32[]{:S(2)}) copy-start(bf16[24]{0:T(256)(128)(2,1)} %param.6) | copy-start | bytes 148
  12.8 17.5 %collective-permute-start = (bf16[1,96,1,8,256]{4,3,2,1,0:T(8,128)(2,1)S(1)}, bf16[1,96,1,8,256]{4,3,2,1,0:T(8,128)(2,1)S(1)}, u32[]{:S(2)}, u32[]{:S(2)}) collective-permute-start(bf16[1,96,1,8,256]{4,3,2,1,0:T(8,128)(2,1)S(1)} %get-tuple-element.35), channel_id=1, source_target_pairs={{0,8},{8,16},{16,24},{24,32},{32,40},{40,48},{48,56},{56,0},{1,9},... | collective-permute-start | bytes 1179656 | tf_op jit(solution)/shard_map/ppermute | solution.py:16
  33.6 30.3 %collective-permute-start.2 = (bf16[1,96,6,1,256]{4,1,3,2,0:T(8,128)(2,1)}, bf16[1,96,6,1,256]{4,1,3,2,0:T(8,128)(2,1)}, u32[]{:S(2)}, u32[]{:S(2)}) collective-permute-start(bf16[1,96,6,1,256]{4,1,3,2,0:T(8,128)(2,1)} %copy.97), channel_id=1, source_target_pairs={{0,1},{1,2},{2,3},{3,4},{4,5},{5,6},{6,7},{7,0},{8,9},{9,10},{10,1... | collective-permute-start | bytes 884744 | tf_op jit(solution)/shard_map/ppermute | solution.py:16
  63.0 8.3 %collective-permute-start.3 = (bf16[1,96,6,1,256]{4,1,3,2,0:T(8,128)(2,1)S(1)}, bf16[1,96,6,1,256]{4,1,3,2,0:T(8,128)(2,1)S(1)}, u32[]{:S(2)}, u32[]{:S(2)}) collective-permute-start(bf16[1,96,6,1,256]{4,1,3,2,0:T(8,128)(2,1)S(1)} %copy.98), channel_id=1, source_target_pairs={{1,0},{2,1},{3,2},{4,3},{5,4},{6,5},{7,6},{0,7},{9,8},{10,9},{11,1... | collective-permute-start | bytes 884744 | tf_op jit(solution)/shard_map/ppermute | solution.py:18
  89.8 3.2 copy-start.3
  89.8 3.2 copy-start.8
  111.7 1.6 copy-start.1
  116.3 90.4 %collective-permute-start.5 = (bf16[1,96,1,8,256]{4,3,2,1,0:T(8,128)(2,1)}, bf16[1,96,1,8,256]{4,3,2,1,0:T(8,128)(2,1)}, u32[]{:S(2)}, u32[]{:S(2)}) collective-permute-start(bf16[1,96,1,8,256]{4,3,2,1,0:T(8,128)(2,1)} %copy.73), channel_id=1, source_target_pairs={{8,0},{16,8},{24,16},{32,24},{40,32},{48,40},{56,48},{0,56},{9,1},... | collective-permute-start | bytes 1179656 | tf_op jit(solution)/shard_map/ppermute | solution.py:18
  117.5 90.7 %collective-permute-start.4 = (bf16[1,96,1,8,256]{4,3,2,1,0:T(8,128)(2,1)}, bf16[1,96,1,8,256]{4,3,2,1,0:T(8,128)(2,1)}, u32[]{:S(2)}, u32[]{:S(2)}) collective-permute-start(bf16[1,96,1,8,256]{4,3,2,1,0:T(8,128)(2,1)} %copy.72), channel_id=1, source_target_pairs={{0,8},{8,16},{16,24},{24,32},{32,40},{40,48},{48,56},{56,0},{1,9},... | collective-permute-start | bytes 1179656 | tf_op jit(solution)/shard_map/ppermute | solution.py:16
  135.9 63.2 %copy-start.2 = (bf16[4,8,8,33,96]{4,2,3,1,0:T(8,128)(2,1)S(1)}, bf16[4,8,8,33,96]{4,2,3,1,0:T(8,128)(2,1)}, u32[]{:S(2)}) copy-start(bf16[4,8,8,33,96]{4,2,3,1,0:T(8,128)(2,1)} %get-tuple-element.21) | copy-start | bytes 4866052
  206.6 175.4 %all-reduce.7.cloned.1.call-start = ((), (), s32[]{:S(2)}) async-start(), calls=%async_computation.1 | async-start | bytes 516096 | tf_op jit(solution)/shard_map/psum | solution.py:93
  210.5 1.6 copy-start
  212.1 6.1 %copy-start.6 = (f32[96]{0:T(128)S(1)}, f32[96]{0:T(128)}, u32[]{:S(2)}) copy-start(f32[96]{0:T(128)} %get-tuple-element.18) | copy-start | bytes 1156
  213.8 19.7 %collective-permute-start.7 = (bf16[1,96,6,1,256]{4,1,3,2,0:T(8,128)(2,1)S(1)}, bf16[1,96,6,1,256]{4,1,3,2,0:T(8,128)(2,1)S(1)}, u32[]{:S(2)}, u32[]{:S(2)}) collective-permute-start(bf16[1,96,6,1,256]{4,1,3,2,0:T(8,128)(2,1)S(1)} %copy.77), channel_id=1, source_target_pairs={{1,0},{2,1},{3,2},{4,3},{5,4},{6,5},{7,6},{0,7},{9,8},{10,9},{11,1... | collective-permute-start | bytes 884744 | tf_op jit(solution)/shard_map/ppermute | solution.py:18
  218.1 15.4 %collective-permute-start.6 = (bf16[1,96,6,1,256]{4,1,3,2,0:T(8,128)(2,1)S(1)}, bf16[1,96,6,1,256]{4,1,3,2,0:T(8,128)(2,1)S(1)}, u32[]{:S(2)}, u32[]{:S(2)}) collective-permute-start(bf16[1,96,6,1,256]{4,1,3,2,0:T(8,128)(2,1)S(1)} %copy.76), channel_id=1, source_target_pairs={{0,1},{1,2},{2,3},{3,4},{4,5},{5,6},{6,7},{7,0},{8,9},{9,10},{10,1... | collective-permute-start | bytes 884744 | tf_op jit(solution)/shard_map/ppermute | solution.py:16
  250.8 3.2 copy-start.4
  250.8 3.2 copy-start.9
Sparse Core Ops, SparseCore 0:
  206.7 25.3 reduce-scatter.3
  303.8 78.1 all-reduce.6
